TPU v7x, 32 devices: a whole 2x2x4 slice. The times are simulated.
32 devices in a mesh: parts: 2 (over y), rows: 4 (over x, core), cols: 4 (over z).
Axes of the slice: x: 2, y: 2, z: 4, core: 2. Of those that a mesh axis runs over, the one named last changes fastest.
Arguments:
- pair: float32 [256, 4, 32, 128], P(('parts', 'rows'), None, 'cols'), parts along dimension 0, may hold values from -6 to 6
- singles: float32 [256, 384], P(('parts', 'rows')), parts along dimension 0, may hold values from -6 to 6
- restype: int32 [256], P(('parts', 'rows')), parts along dimension 0, may hold values from 0 to 31
- block_mask: int32 [32, 4, 4], P(('parts', 'rows'), None, 'cols'), parts along dimension 0, may hold values from 0 to 1, as said below
- ln_trans: float32 [128], replicated, may hold values from 0.1 to 1.9
- w_trans_in: bfloat16 [128, 1024], replicated, may hold values from -0.5 to 0.5
- w_trans_out: bfloat16 [512, 128], replicated, may hold values from -0.25 to 0.25
- ln_bias: float32 [128], replicated, may hold values from 0.1 to 1.9
- w_bias: bfloat16 [128, 16], replicated, may hold values from -0.5 to 0.5
- restype_table: float32 [32, 384], replicated, may hold values from -6 to 6
- ln_single: float32 [384], replicated, may hold values from 0.1 to 1.9
- w_attn: bfloat16 [384, 1536], replicated, may hold values from -80 to 80
- w_single_out: bfloat16 [384, 384], replicated, may hold values from -0.3125 to 0.3125
- w_dist: bfloat16 [128, 64], replicated, may hold values from -0.5 to 0.5
- dist_bias: float32 [64], replicated, may hold values from -6 to 6
Outputs:
- pair_next: float32 [256, 4, 32, 128], P(('parts', 'rows'), None, 'cols'), parts along dimension 0
- singles_next: float32 [256, 384], P(('parts', 'rows')), parts along dimension 0
- dist_logits: float32 [256, 4, 2048], P(('parts', 'rows'), None, 'cols'), parts along dimension 0
There are 2 independent parts, one for each index of `parts`. A program takes and returns all parts, laid end to end along the dimension named above; an argument that names none is the same for every part. Nothing has to cross between parts.
Inputs may be any that keep to these rules, and one draw needn't show every extreme that they name: block_mask[p, a, c] is 1 where p == a * 4 + c.
All inputs are finite; a program needn't handle non-finite values.
Results may differ from a plain program's by a relative error of at most 0.0044.
Values may be sent and summed in bfloat16 or wider, within the bound.
No kernel may reach another device: no remote copies, remote signals or barrier semaphores. Data moves between devices by JAX's collectives and lax.ppermute only.
A program may use at most 64 MiB of HBM per device.

v0:
```python
import math
import jax
import jax.numpy as jnp
from jax import lax
from jax.sharding import PartitionSpec as P

eps_norm = 1e-05


def layer_norm(values, gain_vec):
    average = jnp.mean(values, axis=-1, keepdims=True)
    centred = values - average
    spread = jnp.mean(centred * centred, axis=-1, keepdims=True)
    return centred * lax.rsqrt(spread + eps_norm) * gain_vec


def pair_block(pair_rows, ln_trans, w_trans_in, w_trans_out, ln_bias, w_bias, w_dist):
    hidden_units = w_trans_out.shape[0]
    normed = layer_norm(pair_rows, ln_trans).astype(jnp.bfloat16)
    gate_up = jnp.dot(normed, w_trans_in, preferred_element_type=jnp.float32)
    hidden = (jax.nn.silu(gate_up[:, :hidden_units]) * gate_up[:, hidden_units:]).astype(
        jnp.bfloat16
    )
    updated = pair_rows + jnp.dot(hidden, w_trans_out, preferred_element_type=jnp.float32)
    biased = layer_norm(updated, ln_bias).astype(jnp.bfloat16)
    head_bias = jnp.dot(biased, w_bias, preferred_element_type=jnp.float32)
    binned = jnp.dot(
        updated.astype(jnp.bfloat16), w_dist, preferred_element_type=jnp.float32
    ).astype(jnp.bfloat16)
    return (updated, head_bias, binned)


def local(
    pair,
    singles,
    restype,
    block_mask,
    ln_trans,
    w_trans_in,
    w_trans_out,
    ln_bias,
    w_bias,
    restype_table,
    ln_single,
    w_attn,
    w_single_out,
    w_dist,
    dist_bias,
):
    queries, key_groups, block_len, channels = pair.shape
    key_count = key_groups * block_len
    q_groups = queries // block_len
    head_count = w_bias.shape[1]
    model_width = w_single_out.shape[0]
    head_width = model_width // head_count
    bin_count = w_dist.shape[1]
    step_rows = math.gcd(queries, 16)
    pair_tiles = pair.reshape(queries // step_rows, step_rows * key_count, channels)

    def run_tile(pair_tile):
        return pair_block(pair_tile, ln_trans, w_trans_in, w_trans_out, ln_bias, w_bias, w_dist)

    updated, head_bias, binned = lax.map(run_tile, pair_tiles)
    pair_next = updated.reshape(queries, key_groups, block_len, channels)
    head_bias = head_bias.reshape(queries, key_count, head_count)
    binned = binned.reshape(queries, key_groups, block_len, bin_count)
    type_count = restype_table.shape[0]
    one_hot = (restype[:, None] == jnp.arange(type_count, dtype=jnp.int32)[None, :]).astype(
        jnp.float32
    )
    embedded = singles + jnp.dot(one_hot, restype_table, precision=lax.Precision.HIGHEST)
    normed_s = layer_norm(embedded, ln_single).astype(jnp.bfloat16)
    query_proj = (
        jnp.dot(normed_s, w_attn[:, :model_width], preferred_element_type=jnp.float32)
        * head_width ** (-0.5)
    ).astype(jnp.bfloat16)
    gate_vals = jax.nn.sigmoid(
        jnp.dot(normed_s, w_attn[:, 3 * model_width :], preferred_element_type=jnp.float32)
    )
    key_weights = w_attn[:, model_width : 3 * model_width]
    own_rows = lax.dynamic_slice_in_dim(normed_s, lax.axis_index("cols") * block_len, block_len, 0)
    local_kv = jnp.dot(own_rows, key_weights, preferred_element_type=jnp.float32).astype(
        jnp.bfloat16
    )
    key_values = lax.all_gather(local_kv, "rows", axis=0, tiled=True)
    q_heads = query_proj.reshape(queries, head_count, head_width)
    k_heads = key_values[:, :model_width].reshape(key_count, head_count, head_width)
    v_heads = key_values[:, model_width:].reshape(key_count, head_count, head_width)
    scores = jnp.einsum("qhd,khd->hqk", q_heads, k_heads, preferred_element_type=jnp.float32)
    scores = scores + jnp.transpose(head_bias, (2, 0, 1))
    allowed = (
        jnp.broadcast_to(
            block_mask[:, None, :, :], (q_groups, block_len, key_groups, block_len)
        ).reshape(queries, key_count)
        > 0
    )
    scores = jnp.where(allowed[None], scores, jnp.float32(-1000000000.0))
    local_max = jnp.max(scores, axis=-1)
    row_max = lax.pmax(local_max, "cols")
    expo = jnp.exp(scores - row_max[:, :, None])
    totals = jnp.sum(expo, axis=-1)
    weighted = jnp.einsum(
        "hqk,khd->qhd", expo.astype(jnp.bfloat16), v_heads, preferred_element_type=jnp.float32
    ).reshape(queries, model_width)
    totals, weighted = (
        lax.psum(totals.astype(jnp.bfloat16), "cols").astype(jnp.float32),
        lax.psum(weighted.astype(jnp.bfloat16), "cols").astype(jnp.float32),
    )
    normalised = (
        weighted.reshape(queries, head_count, head_width) / jnp.transpose(totals)[:, :, None]
    )
    attended = (gate_vals * normalised.reshape(queries, model_width)).astype(jnp.bfloat16)
    singles_next = embedded + jnp.dot(attended, w_single_out, preferred_element_type=jnp.float32)
    grouped = binned.reshape(q_groups, block_len, key_groups, block_len * bin_count)
    outgoing = jnp.transpose(grouped, (2, 0, 1, 3)).reshape(
        key_groups * q_groups, 1, block_len, block_len * bin_count
    )
    arrived = lax.all_to_all(outgoing, ("rows", "cols"), split_axis=0, concat_axis=1, tiled=True)
    mirrored = jnp.transpose(
        arrived.reshape(key_groups, q_groups, block_len, block_len, bin_count), (1, 3, 0, 2, 4)
    )
    mirrored = mirrored.reshape(queries, key_groups, block_len, bin_count)
    logits = binned.astype(jnp.float32) + mirrored.astype(jnp.float32) + dist_bias
    dist_logits = logits.reshape(queries, key_groups, block_len * bin_count)
    return (pair_next, singles_next, dist_logits)


def solution(mesh):
    return jax.shard_map(
        local,
        mesh=mesh,
        in_specs=(
            P(("parts", "rows"), None, "cols", None),
            P(("parts", "rows"), None),
            P(("parts", "rows")),
            P(("parts", "rows"), None, "cols"),
            P(),
            P(),
            P(),
            P(),
            P(),
            P(),
            P(),
            P(),
            P(),
            P(),
            P(),
        ),
        out_specs=(
            P(("parts", "rows"), None, "cols", None),
            P(("parts", "rows"), None),
            P(("parts", "rows"), None, "cols"),
        ),
        check_vma=False,
    )
```

profile of v0, /device:TPU:0, one launch (start us, length us, event | category | flops | bytes accessed | tf_op | source)
XLA Modules:
  0.0 56.2 jit_solution(419873935561623359)
XLA Ops:
  0.7 8.1 %while.14 = (s32[]{:T(128)}, f32[2,512,128]{2,1,0:T(8,128)S(1)}, f32[2,512,16]{1,0,2:T(2,128)S(1)}, bf16[2,512,64]{1,2,0:T(8,128)(2,1)S(1)}, f32[2,512,128]{2,1,...) while((s32[]{:T(128)}, f32[2,512,128]{2,1,0:T(8,128)S(1)}, ...), condition=%wide.region_5.6_spmd, body=%wide.region_0.5_spmd.sunk | while | flops 214598656 | bytes 10466621 | solution.py:63
  0.7 1.1 %fusion.65 = (f32[512]{0:T(512)S(1)}, f32[1,512,128]{2,1,0:T(8,128)S(1)}) fusion(f32[2,512,128]{2,1,0:T(8,128)} %get-tuple-element.248, s32[]{:T(128)S(6)} %copy.112), kind=kLoop, calls=%fused_computation.63.clone.1 | loop fusion | flops 65024 | bytes 526340 | tf_op jit(solution)/shard_map/while/body/eval_jaxpr/reduce_sum | solution.py:11
  2.1 0.5 fusion.66
  2.6 0.4 copy-done.14
  3.0 0.5 fusion.67
  3.7 0.4 copy-done.4
  4.1 0.2 convolution_bitcast_fusion.2
  4.4 0.2 dynamic_update_slice.19
  4.8 1.1 %fusion.65 = (f32[512]{0:T(512)S(1)}, f32[1,512,128]{2,1,0:T(8,128)S(1)}) fusion(f32[2,512,128]{2,1,0:T(8,128)} %get-tuple-element.248, s32[]{:T(128)S(6)} %copy.112), kind=kLoop, calls=%fused_computation.63.clone.1 | loop fusion | flops 65024 | bytes 526340 | tf_op jit(solution)/shard_map/while/body/eval_jaxpr/reduce_sum | solution.py:11
  6.2 0.5 fusion.66
  6.7 0.4 copy-done.14
  7.0 0.5 fusion.67
  7.8 0.4 copy-done.4
  8.2 0.2 convolution_bitcast_fusion.2
  8.4 0.2 dynamic_update_slice.19
  8.6 0.2 fusion.68
  8.9 0.2 copy.80
  9.2 0.7 %copy.81 = bf16[4,4,8,512]{3,2,1,0:T(8,128)(2,1)} copy(bf16[4,4,8,512]{3,0,2,1:T(4,128)(2,1)S(1)} %bitcast.74) | data formatting | bytes 262144 | tf_op jit(solution)/shard_map/transpose | solution.py:115
  9.9 7.4 %all-to-all-start = ((bf16[16,1,8,512]{3,2,1,0:T(8,128)(2,1)}), bf16[16,1,8,512]{3,2,1,0:T(8,128)(2,1)S(1)}, u32[]{:S(2)}, u32[]{:S(2)}) async-start(bf16[16,1,8,512]{3,2,1,0:T(8,128)(2,1)} %bitcast.16), calls=%async_computation | async-start | bytes 262144 | tf_op jit(solution)/shard_map/all_to_all | solution.py:118
  17.3 0.3 fusion.38
  17.7 0.2 multiply_reduce_fusion.2
  18.3 0.2 fusion.18
  18.6 0.2 convolution_convert_fusion.2
  18.7 5.3 %all_gather.3 = bf16[32,768]{1,0:T(8,128)(2,1)S(1)} all-gather(bf16[8,768]{1,0:T(8,128)(2,1)S(1)} %convolution_convert_fusion.2), channel_id=1, replica_groups=mesh['parts'=2,'rows'=4,'cols'=4] {'rows'}, dimensions={0}, use_global_device_ids=true | all-gather | bytes 61440 | tf_op jit(solution)/shard_map/all_gather | solution.py:85
  24.5 0.3 fusion.39
  24.8 12.1 %pmax.7 = f32[16,32]{1,0:T(8,128)S(1)} all-reduce(f32[16,32]{1,0:T(8,128)S(1)} %get-tuple-element.141), channel_id=1, replica_groups=mesh['parts'=2,'rows'=4,'cols'=4] {'cols'}, use_global_device_ids=true, to_apply=%region_9.10 | all-reduce | flops 512 | bytes 4096 | tf_op jit(solution)/shard_map/pmax | solution.py:99
  37.0 0.2 convolution_convert_fusion.1
  37.6 15.8 %all-reduce = (bf16[32,16]{0,1:T(8,128)(2,1)S(1)}, bf16[32,384]{1,0:T(8,128)(2,1)S(1)}) all-reduce(bf16[32,16]{0,1:T(8,128)(2,1)S(1)} %bitcast.79, bf16[32,384]{1,0:T(8,128)(2,1)S(1)} %copy.89), channel_id=1, replica_groups=mesh['parts'=2,'rows'=4,'cols'=4] {'cols'}, use_global_device_ids=true, to_apply=%region_12.13 | all-reduce | flops 12800 | bytes 51200 | tf_op jit(solution)/shard_map/psum | solution.py:106
  53.7 0.2 reshape.110
  54.0 1.0 %convolution_add_fusion.3 = f32[32,384]{1,0:T(8,128)} fusion(f32[32,384]{1,0:T(8,128)S(1)} %get-tuple-element.140, bf16[384,384]{1,0:T(8,128)(2,1)S(1)} %copy-done, bf16[32,384]{1,0:T(8,128)(2,1)S(1)} %multiply_convert_fusion.4, bf16[384,1536]{1,0:T(8,128)(2,1)S(1)} %copy-done.2, f32[32,384]{1,0:T(8,128)S(1)} %div.40, ...), kind=kOutput, calls=%fused_computation.36 | convolution fusion | flops 18972672 | bytes 786432 | tf_op jit(solution)/shard_map/dot_general | solution.py:113
  55.2 0.2 reshape.111
  55.4 0.8 %add_add_fusion = f32[32,4,512]{2,1,0:T(4,128)} fusion(f32[32,4,512]{2,1,0:T(4,128)S(1)} %reshape.110, f32[32,4,512]{2,1,0:T(4,128)S(1)} %reshape.111, f32[512]{0:T(512)S(1)} %add.82), kind=kLoop, calls=%fused_computation.44 | loop fusion | flops 131072 | bytes 788480 | tf_op jit(solution)/shard_map/add | solution.py:123
  (87 shorter events, 3.3 us)
Async XLA Ops:
  0.6 53.4 %copy-start = (bf16[384,384]{1,0:T(8,128)(2,1)S(1)}, bf16[384,384]{1,0:T(8,128)(2,1)}, u32[]{:S(2)}) copy-start(bf16[384,384]{1,0:T(8,128)(2,1)} %param.29) | copy-start | bytes 884740
  0.7 1.4 %copy-start.1 = (bf16[128,1024]{1,0:T(8,128)(2,1)S(1)}, bf16[128,1024]{1,0:T(8,128)(2,1)}, u32[]{:S(2)}) copy-start(bf16[128,1024]{1,0:T(8,128)(2,1)} %get-tuple-element.250) | copy-start | bytes 786436 | tf_op jit(solution)/shard_map/while
  0.7 1.4 %copy-start.8 = (f32[128]{0:T(128)S(1)}, f32[128]{0:T(128)}, u32[]{:S(2)}) copy-start(f32[128]{0:T(128)} %get-tuple-element.249) | copy-start | bytes 1540 | tf_op jit(solution)/shard_map/while
  2.1 0.9 %copy-start.14 = (bf16[512,128]{1,0:T(8,128)(2,1)S(1)}, bf16[512,128]{1,0:T(8,128)(2,1)}, u32[]{:S(2)}) copy-start(bf16[512,128]{1,0:T(8,128)(2,1)} %get-tuple-element.251) | copy-start | bytes 393220 | tf_op jit(solution)/shard_map/while
  3.5 0.7 %copy-start.4 = (bf16[128,16]{0,1:T(8,128)(2,1)S(1)}, bf16[128,16]{0,1:T(8,128)(2,1)}, u32[]{:S(2)}) copy-start(bf16[128,16]{0,1:T(8,128)(2,1)} %get-tuple-element.253) | copy-start | bytes 12292 | tf_op jit(solution)/shard_map/while
  3.5 0.7 %copy-start.7 = (f32[128]{0:T(128)S(1)}, f32[128]{0:T(128)}, u32[]{:S(2)}) copy-start(f32[128]{0:T(128)} %get-tuple-element.252) | copy-start | bytes 1540 | tf_op jit(solution)/shard_map/while
  3.5 1.1 %copy-start.3 = (bf16[128,64]{0,1:T(8,128)(2,1)S(1)}, bf16[128,64]{0,1:T(8,128)(2,1)}, u32[]{:S(2)}) copy-start(bf16[128,64]{0,1:T(8,128)(2,1)} %get-tuple-element.254) | copy-start | bytes 49156 | tf_op jit(solution)/shard_map/while
  4.7 1.4 %copy-start.1 = (bf16[128,1024]{1,0:T(8,128)(2,1)S(1)}, bf16[128,1024]{1,0:T(8,128)(2,1)}, u32[]{:S(2)}) copy-start(bf16[128,1024]{1,0:T(8,128)(2,1)} %get-tuple-element.250) | copy-start | bytes 786436 | tf_op jit(solution)/shard_map/while
  4.8 1.4 %copy-start.8 = (f32[128]{0:T(128)S(1)}, f32[128]{0:T(128)}, u32[]{:S(2)}) copy-start(f32[128]{0:T(128)} %get-tuple-element.249) | copy-start | bytes 1540 | tf_op jit(solution)/shard_map/while
  6.1 0.9 %copy-start.14 = (bf16[512,128]{1,0:T(8,128)(2,1)S(1)}, bf16[512,128]{1,0:T(8,128)(2,1)}, u32[]{:S(2)}) copy-start(bf16[512,128]{1,0:T(8,128)(2,1)} %get-tuple-element.251) | copy-start | bytes 393220 | tf_op jit(solution)/shard_map/while
  7.5 0.7 %copy-start.4 = (bf16[128,16]{0,1:T(8,128)(2,1)S(1)}, bf16[128,16]{0,1:T(8,128)(2,1)}, u32[]{:S(2)}) copy-start(bf16[128,16]{0,1:T(8,128)(2,1)} %get-tuple-element.253) | copy-start | bytes 12292 | tf_op jit(solution)/shard_map/while
  7.5 0.7 %copy-start.7 = (f32[128]{0:T(128)S(1)}, f32[128]{0:T(128)}, u32[]{:S(2)}) copy-start(f32[128]{0:T(128)} %get-tuple-element.252) | copy-start | bytes 1540 | tf_op jit(solution)/shard_map/while
  7.5 1.1 %copy-start.3 = (bf16[128,64]{0,1:T(8,128)(2,1)S(1)}, bf16[128,64]{0,1:T(8,128)(2,1)}, u32[]{:S(2)}) copy-start(bf16[128,64]{0,1:T(8,128)(2,1)} %get-tuple-element.254) | copy-start | bytes 49156 | tf_op jit(solution)/shard_map/while
  8.8 9.4 %copy-start.13 = (f32[2,512,128]{2,1,0:T(8,128)}, f32[2,512,128]{2,1,0:T(8,128)S(1)}, u32[]{:S(2)}) copy-start(f32[2,512,128]{2,1,0:T(8,128)S(1)} %get-tuple-element.62) | copy-start | bytes 1572868
  8.8 8.5 %copy-start.5 = (f32[32,384]{1,0:T(8,128)S(1)}, f32[32,384]{1,0:T(8,128)}, u32[]{:S(2)}) copy-start(f32[32,384]{1,0:T(8,128)} %param.18) | copy-start | bytes 147460
  8.8 8.5 %copy-start.6 = (f32[32,384]{1,0:T(8,128)S(1)}, f32[32,384]{1,0:T(8,128)}, u32[]{:S(2)}) copy-start(f32[32,384]{1,0:T(8,128)} %param.26) | copy-start | bytes 147460
  8.8 8.5 %copy-start.11 = (s32[32]{0:T(128)S(1)}, s32[32]{0:T(128)}, u32[]{:S(2)}) copy-start(s32[32]{0:T(128)} %param.19) | copy-start | bytes 388
  8.8 9.3 %copy-start.9 = (f32[384]{0:T(512)S(1)}, f32[384]{0:T(512)}, u32[]{:S(2)}) copy-start(f32[384]{0:T(512)} %param.27) | copy-start | bytes 4612
  8.8 9.4 %copy-start.2 = (bf16[384,1536]{1,0:T(8,128)(2,1)S(1)}, bf16[384,1536]{1,0:T(8,128)(2,1)}, u32[]{:S(2)}) copy-start(bf16[384,1536]{1,0:T(8,128)(2,1)} %param.28) | copy-start | bytes 3538948
  9.9 45.1 %all-to-all-start = ((bf16[16,1,8,512]{3,2,1,0:T(8,128)(2,1)}), bf16[16,1,8,512]{3,2,1,0:T(8,128)(2,1)S(1)}, u32[]{:S(2)}, u32[]{:S(2)}) async-start(bf16[16,1,8,512]{3,2,1,0:T(8,128)(2,1)} %bitcast.16), calls=%async_computation | async-start | bytes 262144 | tf_op jit(solution)/shard_map/all_to_all | solution.py:118
  17.6 6.6 %copy-start.10 = (s32[4,4,1]{1,2,0:T(1,128)S(1)}, s32[4,4,1]{1,2,0:T(1,128)}, u32[]{:S(2)}) copy-start(s32[4,4,1]{1,2,0:T(1,128)} %param.20) | copy-start | bytes 196
  37.3 16.7 %copy-start.12 = (f32[64]{0:T(128)S(1)}, f32[64]{0:T(128)}, u32[]{:S(2)}) copy-start(f32[64]{0:T(128)} %param.31) | copy-start | bytes 772
where the time goes:
time: 56.6 us; the launch traced here: 56.2 us
  blocking collectives  33.3 us (59%)
  starting transfers between devices  7.39 us (13%)
  local copies, waits for them, and re-layouts  5.89 us (10%)
  matrix products  4.73 us (8%)
  other arithmetic  3.66 us (6%)
  between operations  0.96 us (2%)
    psum x1, blocking collectives, local(): lax.psum(totals.astype(jnp.bfloat16), 'cols').astype(jnp.float32)  15.8 us
    pmax x1, blocking collectives, local(): row_max = lax.pmax(local_max, 'cols')  12.1 us
    all_to_all x1, starting transfers between devices, local(): lax.all_to_all(outgoing, ('rows', 'cols'), split_axis=0, concat_axis=1, t...  7.39 us
    all_gather x1, blocking collectives, local(): key_values = lax.all_gather(local_kv, 'rows', axis=0, tiled=True)  5.33 us
    reduce_sum x2, other arithmetic, layer_norm(): average = jnp.mean(values, axis=-1, keepdims=True)  2.28 us
    while x24, local copies, waits for them, and re-layouts  1.65 us
  transfers between devices with their start and end apart: 1, of which 0 were waited for; matrix products, arithmetic and copies ran while one was open for 7% of the time, Pallas kernels for 0%

commit v1 on v0

--- a/solution.py
+++ b/solution.py
@@ -103,7 +103,7 @@
         "hqk,khd->qhd", expo.astype(jnp.bfloat16), v_heads, preferred_element_type=jnp.float32
     ).reshape(queries, model_width)
     totals, weighted = (
-        lax.psum(totals.astype(jnp.bfloat16), "cols").astype(jnp.float32),
+        jnp.sum(lax.all_gather(totals.astype(jnp.bfloat16), "cols"), axis=0).astype(jnp.float32),
         lax.psum(weighted.astype(jnp.bfloat16), "cols").astype(jnp.float32),
     )
     normalised = (

time: 56.6 us -> 69.8 us (1.23)
  blocking collectives: 33.3 us -> 46.5 us
    all_gather x0 -> x1, blocking collectives: none -> 13.2 us  [local(): lax.all_gather(totals.astype(jnp.bfloat16), 'cols')]
  transfers between devices with their start and end apart: 1 -> 1, of which waited for: 0 -> 0; matrix products, arithmetic and copies ran while one was open for 7% -> 6% of each run, Pallas kernels for 0% -> 0%
where the time goes in v1:
time: 69.8 us; the launch traced here: 69.4 us
  blocking collectives  46.5 us (67%)
  starting transfers between devices  7.39 us (11%)
  local copies, waits for them, and re-layouts  5.89 us (8%)
  matrix products  4.74 us (7%)
  other arithmetic  3.67 us (5%)
  between operations  0.97 us (1%)
    psum x1, blocking collectives, local(): lax.psum(weighted.astype(jnp.bfloat16), 'cols').astype(jnp.float32)  15.8 us
    all_gather x1, blocking collectives, local(): lax.all_gather(totals.astype(jnp.bfloat16), 'cols')  13.2 us
    pmax x1, blocking collectives, local(): row_max = lax.pmax(local_max, 'cols')  12.1 us
    all_to_all x1, starting transfers between devices, local(): lax.all_to_all(outgoing, ('rows', 'cols'), split_axis=0, concat_axis=1, t...  7.39 us
    all_gather x1, blocking collectives, local(): key_values = lax.all_gather(local_kv, 'rows', axis=0, tiled=True)  5.33 us
    reduce_sum x2, other arithmetic, layer_norm(): average = jnp.mean(values, axis=-1, keepdims=True)  2.28 us
    while x24, local copies, waits for them, and re-layouts  1.65 us
  transfers between devices with their start and end apart: 1, of which 0 were waited for; matrix products, arithmetic and copies ran while one was open for 6% of the time, Pallas kernels for 0%

profile of v1, /device:TPU:0, one launch (start us, length us, event | category | flops | bytes accessed | tf_op | source)
XLA Modules:
  0.0 69.4 jit_solution(15048913761642670604)
XLA Ops:
  0.7 8.1 %while.14 = (s32[]{:T(128)}, f32[2,512,128]{2,1,0:T(8,128)S(1)}, f32[2,512,16]{1,0,2:T(2,128)S(1)}, bf16[2,512,64]{1,2,0:T(8,128)(2,1)S(1)}, f32[2,512,128]{2,1,...) while((s32[]{:T(128)}, f32[2,512,128]{2,1,0:T(8,128)S(1)}, ...), condition=%wide.region_5.6_spmd, body=%wide.region_0.5_spmd.sunk | while | flops 214598656 | bytes 10466621 | solution.py:63
  0.7 1.1 %fusion.65 = (f32[512]{0:T(512)S(1)}, f32[1,512,128]{2,1,0:T(8,128)S(1)}) fusion(f32[2,512,128]{2,1,0:T(8,128)} %get-tuple-element.246, s32[]{:T(128)S(6)} %copy.112), kind=kLoop, calls=%fused_computation.63.clone.1 | loop fusion | flops 65024 | bytes 526340 | tf_op jit(solution)/shard_map/while/body/eval_jaxpr/reduce_sum | solution.py:11
  2.1 0.5 fusion.66
  2.6 0.4 copy-done.14
  3.0 0.5 fusion.67
  3.7 0.4 copy-done.4
  4.1 0.2 convolution_bitcast_fusion.2
  4.4 0.2 dynamic_update_slice.19
  4.8 1.1 %fusion.65 = (f32[512]{0:T(512)S(1)}, f32[1,512,128]{2,1,0:T(8,128)S(1)}) fusion(f32[2,512,128]{2,1,0:T(8,128)} %get-tuple-element.246, s32[]{:T(128)S(6)} %copy.112), kind=kLoop, calls=%fused_computation.63.clone.1 | loop fusion | flops 65024 | bytes 526340 | tf_op jit(solution)/shard_map/while/body/eval_jaxpr/reduce_sum | solution.py:11
  6.2 0.5 fusion.66
  6.7 0.4 copy-done.14
  7.0 0.5 fusion.67
  7.8 0.4 copy-done.4
  8.2 0.2 convolution_bitcast_fusion.2
  8.4 0.2 dynamic_update_slice.19
  8.9 0.2 copy.80
  9.2 0.7 copy.81
  9.9 7.4 %all-to-all-start = ((bf16[16,1,8,512]{3,2,1,0:T(8,128)(2,1)}), bf16[16,1,8,512]{3,2,1,0:T(8,128)(2,1)S(1)}, u32[]{:S(2)}, u32[]{:S(2)}) async-start(bf16[16,1,8,512]{3,2,1,0:T(8,128)(2,1)} %bitcast.17), calls=%async_computation | async-start | bytes 262144 | tf_op jit(solution)/shard_map/all_to_all | solution.py:118
  17.3 0.3 fusion.38
  17.7 0.2 multiply_reduce_fusion.2
  18.3 0.2 fusion.18
  18.6 0.2 convolution_convert_fusion.2
  18.7 5.3 %all_gather.7 = bf16[32,768]{1,0:T(8,128)(2,1)S(1)} all-gather(bf16[8,768]{1,0:T(8,128)(2,1)S(1)} %convolution_convert_fusion.2), channel_id=1, replica_groups=mesh['parts'=2,'rows'=4,'cols'=4] {'rows'}, dimensions={0}, use_global_device_ids=true | all-gather | bytes 61440 | tf_op jit(solution)/shard_map/all_gather | solution.py:85
  24.5 0.3 fusion.39
  24.8 12.1 %pmax.7 = f32[16,32]{1,0:T(8,128)S(1)} all-reduce(f32[16,32]{1,0:T(8,128)S(1)} %get-tuple-element.139), channel_id=1, replica_groups=mesh['parts'=2,'rows'=4,'cols'=4] {'cols'}, use_global_device_ids=true, to_apply=%region_9.10 | all-reduce | flops 512 | bytes 4096 | tf_op jit(solution)/shard_map/pmax | solution.py:99
  37.0 13.2 %all-gather = bf16[64,32]{1,0:T(8,128)(2,1)S(1)} all-gather(bf16[16,32]{1,0:T(8,128)(2,1)S(1)} %fusion.24), channel_id=2, replica_groups=mesh['parts'=2,'rows'=4,'cols'=4] {'cols'}, dimensions={0}, use_global_device_ids=true | all-gather | bytes 5120 | tf_op jit(solution)/shard_map/all_gather | solution.py:106
  50.4 0.2 convolution_convert_fusion.1
  50.7 15.8 %psum.7 = bf16[32,384]{1,0:T(8,128)(2,1)S(1)} all-reduce(bf16[32,384]{1,0:T(8,128)(2,1)S(1)} %copy.89), channel_id=1, replica_groups=mesh['parts'=2,'rows'=4,'cols'=4] {'cols'}, use_global_device_ids=true, to_apply=%region_10.11 | all-reduce | flops 12288 | bytes 49152 | tf_op jit(solution)/shard_map/psum | solution.py:107
  66.9 0.2 reshape.118
  67.2 1.0 %convolution_add_fusion.3 = f32[32,384]{1,0:T(8,128)} fusion(f32[32,384]{1,0:T(8,128)S(1)} %get-tuple-element.138, bf16[384,384]{1,0:T(8,128)(2,1)S(1)} %copy-done, bf16[32,384]{1,0:T(8,128)(2,1)S(1)} %multiply_convert_fusion.4, bf16[384,1536]{1,0:T(8,128)(2,1)S(1)} %copy-done.2, f32[32,384]{1,0:T(8,128)S(1)} %div.40, bf16[32,384]{1,0:T(8,128)(2,1)S(1)} %psum.7), kind=kOutput, calls=%fused_computation.36 | convolution fusion | flops 18972672 | bytes 786432 | tf_op jit(solution)/shard_map/dot_general | solution.py:113
  68.4 0.2 reshape.119
  68.6 0.8 %add_add_fusion = f32[32,4,512]{2,1,0:T(4,128)} fusion(f32[32,4,512]{2,1,0:T(4,128)S(1)} %reshape.118, f32[32,4,512]{2,1,0:T(4,128)S(1)} %reshape.119, f32[512]{0:T(512)S(1)} %add.80), kind=kLoop, calls=%fused_computation.44 | loop fusion | flops 131072 | bytes 788480 | tf_op jit(solution)/shard_map/add | solution.py:123
  (90 shorter events, 3.5 us)
Async XLA Ops:
  0.6 66.6 %copy-start = (bf16[384,384]{1,0:T(8,128)(2,1)S(1)}, bf16[384,384]{1,0:T(8,128)(2,1)}, u32[]{:S(2)}) copy-start(bf16[384,384]{1,0:T(8,128)(2,1)} %param.29) | copy-start | bytes 884740
  0.7 1.4 %copy-start.1 = (bf16[128,1024]{1,0:T(8,128)(2,1)S(1)}, bf16[128,1024]{1,0:T(8,128)(2,1)}, u32[]{:S(2)}) copy-start(bf16[128,1024]{1,0:T(8,128)(2,1)} %get-tuple-element.248) | copy-start | bytes 786436 | tf_op jit(solution)/shard_map/while
  0.7 1.4 %copy-start.8 = (f32[128]{0:T(128)S(1)}, f32[128]{0:T(128)}, u32[]{:S(2)}) copy-start(f32[128]{0:T(128)} %get-tuple-element.247) | copy-start | bytes 1540 | tf_op jit(solution)/shard_map/while
  2.1 0.9 %copy-start.14 = (bf16[512,128]{1,0:T(8,128)(2,1)S(1)}, bf16[512,128]{1,0:T(8,128)(2,1)}, u32[]{:S(2)}) copy-start(bf16[512,128]{1,0:T(8,128)(2,1)} %get-tuple-element.249) | copy-start | bytes 393220 | tf_op jit(solution)/shard_map/while
  3.5 0.7 copy-start.4
  3.5 0.7 copy-start.7
  3.5 1.1 %copy-start.3 = (bf16[128,64]{0,1:T(8,128)(2,1)S(1)}, bf16[128,64]{0,1:T(8,128)(2,1)}, u32[]{:S(2)}) copy-start(bf16[128,64]{0,1:T(8,128)(2,1)} %get-tuple-element.252) | copy-start | bytes 49156 | tf_op jit(solution)/shard_map/while
  4.7 1.4 %copy-start.1 = (bf16[128,1024]{1,0:T(8,128)(2,1)S(1)}, bf16[128,1024]{1,0:T(8,128)(2,1)}, u32[]{:S(2)}) copy-start(bf16[128,1024]{1,0:T(8,128)(2,1)} %get-tuple-element.248) | copy-start | bytes 786436 | tf_op jit(solution)/shard_map/while
  4.8 1.4 %copy-start.8 = (f32[128]{0:T(128)S(1)}, f32[128]{0:T(128)}, u32[]{:S(2)}) copy-start(f32[128]{0:T(128)} %get-tuple-element.247) | copy-start | bytes 1540 | tf_op jit(solution)/shard_map/while
  6.1 0.9 %copy-start.14 = (bf16[512,128]{1,0:T(8,128)(2,1)S(1)}, bf16[512,128]{1,0:T(8,128)(2,1)}, u32[]{:S(2)}) copy-start(bf16[512,128]{1,0:T(8,128)(2,1)} %get-tuple-element.249) | copy-start | bytes 393220 | tf_op jit(solution)/shard_map/while
  7.5 0.7 copy-start.4
  7.5 0.7 copy-start.7
  7.5 1.1 %copy-start.3 = (bf16[128,64]{0,1:T(8,128)(2,1)S(1)}, bf16[128,64]{0,1:T(8,128)(2,1)}, u32[]{:S(2)}) copy-start(bf16[128,64]{0,1:T(8,128)(2,1)} %get-tuple-element.252) | copy-start | bytes 49156 | tf_op jit(solution)/shard_map/while
  8.8 9.4 %copy-start.13 = (f32[2,512,128]{2,1,0:T(8,128)}, f32[2,512,128]{2,1,0:T(8,128)S(1)}, u32[]{:S(2)}) copy-start(f32[2,512,128]{2,1,0:T(8,128)S(1)} %get-tuple-element.62) | copy-start | bytes 1572868
  8.8 8.5 %copy-start.5 = (f32[32,384]{1,0:T(8,128)S(1)}, f32[32,384]{1,0:T(8,128)}, u32[]{:S(2)}) copy-start(f32[32,384]{1,0:T(8,128)} %param.18) | copy-start | bytes 147460
  8.8 8.5 %copy-start.6 = (f32[32,384]{1,0:T(8,128)S(1)}, f32[32,384]{1,0:T(8,128)}, u32[]{:S(2)}) copy-start(f32[32,384]{1,0:T(8,128)} %param.26) | copy-start | bytes 147460
  8.8 8.5 %copy-start.11 = (s32[32]{0:T(128)S(1)}, s32[32]{0:T(128)}, u32[]{:S(2)}) copy-start(s32[32]{0:T(128)} %param.19) | copy-start | bytes 388
  8.8 9.3 %copy-start.9 = (f32[384]{0:T(512)S(1)}, f32[384]{0:T(512)}, u32[]{:S(2)}) copy-start(f32[384]{0:T(512)} %param.27) | copy-start | bytes 4612
  8.8 9.4 %copy-start.2 = (bf16[384,1536]{1,0:T(8,128)(2,1)S(1)}, bf16[384,1536]{1,0:T(8,128)(2,1)}, u32[]{:S(2)}) copy-start(bf16[384,1536]{1,0:T(8,128)(2,1)} %param.28) | copy-start | bytes 3538948
  9.9 58.3 %all-to-all-start = ((bf16[16,1,8,512]{3,2,1,0:T(8,128)(2,1)}), bf16[16,1,8,512]{3,2,1,0:T(8,128)(2,1)S(1)}, u32[]{:S(2)}, u32[]{:S(2)}) async-start(bf16[16,1,8,512]{3,2,1,0:T(8,128)(2,1)} %bitcast.17), calls=%async_computation | async-start | bytes 262144 | tf_op jit(solution)/shard_map/all_to_all | solution.py:118
  17.6 6.6 %copy-start.10 = (s32[4,4,1]{1,2,0:T(1,128)S(1)}, s32[4,4,1]{1,2,0:T(1,128)}, u32[]{:S(2)}) copy-start(s32[4,4,1]{1,2,0:T(1,128)} %param.20) | copy-start | bytes 196
  50.6 16.6 %copy-start.12 = (f32[64]{0:T(128)S(1)}, f32[64]{0:T(128)}, u32[]{:S(2)}) copy-start(f32[64]{0:T(128)} %param.31) | copy-start | bytes 772
